TPU v7x, 32 devices: a whole 2x2x4 slice. The times are simulated.
32 devices in a mesh: groups: 2 (over y), seq: 4 (over z), tile: 2 (over x), chan: 2 (over core).
Axes of the slice: x: 2, y: 2, z: 4, core: 2. Of those that a mesh axis runs over, the one named last changes fastest.
Arguments:
- latents: bfloat16 [2, 7680, 384], P('tile', ('groups', 'seq'), 'chan'), parts along dimension 1, may hold values from -6 to 6
- norm_gain: float32 [384], replicated, may hold values from 0.1 to 1.9
- conv_weight: bfloat16 [3, 3, 3, 384, 384], P(None, None, None, None, 'chan'), may hold values from -0.0625 to 0.0625
- conv_bias: float32 [384], P('chan'), may hold values from -3 to 3
- upsample_weight: bfloat16 [3, 3, 384, 192], P(None, None, None, 'chan'), may hold values from -0.109375 to 0.109375
- upsample_bias: float32 [192], P('chan'), may hold values from -3 to 3
Outputs:
- decoded: bfloat16 [8, 192, 20, 384], P(None, ('groups', 'tile'), 'seq', 'chan'), parts along dimension 1
There are 2 independent parts, one for each index of `groups`. A program takes and returns all parts, laid end to end along the dimension named above; an argument that names none is the same for every part. Nothing has to cross between parts.
All inputs are finite; a program needn't handle non-finite values.
Results may differ from a plain program's by a relative error of at most 0.005.
Values may be sent and summed in bfloat16 or wider, within the bound.
No kernel may reach another device: no remote copies, remote signals or barrier semaphores. Data moves between devices by JAX's collectives and lax.ppermute only.
A program may use at most 64 MiB of HBM per device.

v0:
```python
import jax
import jax.numpy as jnp
from jax import lax
from jax.sharding import PartitionSpec as P

FRAMES = 8
ROWS_DEV = 24
COLS_DEV = 5
norm_eps = 1e-06


def extended(cells, sides, width):
    for axis, dim in sides:
        count = lax.axis_size(axis)
        ends = count - 1
        head = lax.slice_in_dim(cells, 0, width, axis=dim)
        tail = lax.slice_in_dim(cells, cells.shape[dim] - width, cells.shape[dim], axis=dim)
        cells = jnp.concatenate(
            [
                lax.ppermute(tail, axis, [(i, (i + 1) % count) for i in range(ends)]),
                cells,
                lax.ppermute(head, axis, [((i + 1) % count, i) for i in range(ends)]),
            ],
            axis=dim,
        )
    return cells


def activate(padded, norm_gain):
    values = padded.astype(jnp.float32)
    scale = lax.rsqrt(jnp.mean(values * values, axis=-1, keepdims=True) + norm_eps)
    return jax.nn.silu(values * scale * norm_gain).astype(jnp.bfloat16)


def body(latents, norm_gain, conv_weight, conv_bias, upsample_weight, upsample_bias):
    seq_count = lax.axis_size("seq")
    local_chan = conv_bias.shape[0]
    rows_src = FRAMES * ROWS_DEV // seq_count
    whole = lax.all_gather(latents[0], "chan", axis=1, tiled=True)
    arranged = whole.reshape(rows_src, seq_count, COLS_DEV, whole.shape[1])
    regrouped = lax.all_to_all(arranged, "seq", split_axis=1, concat_axis=0, tiled=True)
    full_field = regrouped.reshape(FRAMES, ROWS_DEV, COLS_DEV, whole.shape[1])
    padded = extended(full_field, (("seq", 2), ("tile", 1)), 1)
    field_own = lax.dynamic_slice_in_dim(
        full_field, lax.axis_index("chan") * local_chan, local_chan, 3
    )
    activation = activate(padded, norm_gain)
    shifted = jnp.pad(activation, ((2, 0), (0, 0), (0, 0), (0, 0)))
    conv_out = lax.conv_general_dilated(
        shifted[None],
        conv_weight,
        (1, 1, 1),
        "VALID",
        dimension_numbers=("NDHWC", "DHWIO", "NDHWC"),
        preferred_element_type=jnp.float32,
    )[0]
    middle = (field_own.astype(jnp.float32) + conv_out + conv_bias).astype(jnp.bfloat16)
    middle_rim = extended(middle, (("seq", 2), ("tile", 1)), 1)
    middle_full = lax.all_gather(middle_rim, "chan", axis=3, tiled=True)
    upsampled = jnp.repeat(jnp.repeat(middle_full, 2, axis=1), 2, axis=2)[:, 1:-1, 1:-1, :]
    image = lax.conv_general_dilated(
        upsampled,
        upsample_weight,
        (1, 1),
        "VALID",
        dimension_numbers=("NHWC", "HWIO", "NHWC"),
        preferred_element_type=jnp.float32,
    )
    image = image + upsample_bias
    out_chan = upsample_bias.shape[0]
    image = image.reshape(FRAMES, 2 * ROWS_DEV, COLS_DEV, 2, out_chan)
    image = jnp.transpose(image, (0, 1, 2, 4, 3)).reshape(
        FRAMES, 2 * ROWS_DEV, COLS_DEV, 2 * out_chan
    )
    return image.astype(jnp.bfloat16)


def solution(mesh):
    in_specs = (
        P("tile", ("groups", "seq"), "chan"),
        P(),
        P(None, None, None, None, "chan"),
        P("chan"),
        P(None, None, None, "chan"),
        P("chan"),
    )
    out_specs = P(None, ("groups", "tile"), "seq", "chan")
    return jax.shard_map(body, mesh=mesh, in_specs=in_specs, out_specs=out_specs, check_vma=False)
```

profile of v0, /device:TPU:0, one launch (start us, length us, event | category | flops | bytes accessed | tf_op | source)
XLA Modules:
  0.0 154.0 jit_solution(12144148786594133457)
XLA Ops:
  6.5 0.0 copy-start
  6.5 0.0 all-gather.3.cloned.1.call-start
  6.5 2.8 %all-gather = bf16[1,960,384]{1,2,0:T(8,128)(2,1)S(1)} all-gather(bf16[1,960,192]{1,2,0:T(8,128)(2,1)} %param.6), channel_id=2, replica_groups=mesh['groups'=2,'seq'=4,'tile'=2,'chan'=2] {'chan'}, dimensions={2}, use_global_device_ids=true | all-gather | bytes 1105920 | tf_op jit(solution)/shard_map/all_gather | solution.py:39
  9.4 0.4 copy.26
  9.7 0.3 reshape.28
  10.0 0.3 copy.27
  10.3 0.0 copy-start.1
  10.3 25.4 %all_to_all.15 = bf16[48,4,5,384]{3,0,2,1:T(8,128)(2,1)S(1)} all-to-all(bf16[48,4,5,384]{3,0,2,1:T(8,128)(2,1)S(1)} %copy.27), channel_id=1, replica_groups=mesh['groups'=2,'seq'=4,'tile'=2,'chan'=2] {'seq'}, dimensions={1} | all-to-all | bytes 1474560 | tf_op jit(solution)/shard_map/all_to_all | solution.py:41
  35.7 0.1 copy.28
  35.8 2.3 %collective-permute-start = (bf16[8,24,1,384]{3,1,0,2:T(8,128)(2,1)S(1)}, bf16[8,24,1,384]{3,1,0,2:T(8,128)(2,1)S(1)}, u32[]{:S(2)}, u32[]{:S(2)}) collective-permute-start(bf16[8,24,1,384]{3,1,0,2:T(8,128)(2,1)S(1)} %get-tuple-element.7), channel_id=1, source_target_pairs={{0,4},{4,8},{8,12},{1,5},{5,9},{9,13},{2,6},{6,10},{10,14},{3,7},{... | collective-permute-start | bytes 442376 | tf_op jit(solution)/shard_map/ppermute | solution.py:20
  38.1 1.3 collective-permute-start.1
  39.4 1.3 collective-permute-done
  40.7 4.4 %collective-permute-done.1 = bf16[8,24,1,384]{3,1,0,2:T(8,128)(2,1)S(1)} collective-permute-done((bf16[8,24,1,384]{3,1,0,2:T(8,128)(2,1)S(1)}, bf16[8,24,1,384]{3,1,0,2:T(8,128)(2,1)S(1)}, u32[]{:S(2)}, u32[]{:S(2)}) %collective-permute-start.1) | collective-permute-done | bytes 147488 | tf_op jit(solution)/shard_map/ppermute | solution.py:22
  45.1 0.1 pad_maximum_fusion.4
  45.3 3.4 %collective-permute-start.2 = (bf16[8,1,7,384]{3,1,0,2:T(2,128)(2,1)S(1)}, bf16[8,1,7,384]{3,1,0,2:T(2,128)(2,1)S(1)}, u32[]{:S(2)}, u32[]{:S(2)}) collective-permute-start(bf16[8,1,7,384]{3,1,0,2:T(2,128)(2,1)S(1)} %get-tuple-element.5), channel_id=1, source_target_pairs={{0,2},{1,3},{4,6},{5,7},{8,10},{9,11},{12,14},{13,15},{16,18},{17,... | collective-permute-start | bytes 129032 | tf_op jit(solution)/shard_map/ppermute | solution.py:20
  48.7 1.3 collective-permute-start.3
  50.0 0.8 collective-permute-done.2
  50.8 4.3 %collective-permute-done.3 = bf16[8,1,7,384]{3,1,0,2:T(2,128)(2,1)S(1)} collective-permute-done((bf16[8,1,7,384]{3,1,0,2:T(2,128)(2,1)S(1)}, bf16[8,1,7,384]{3,1,0,2:T(2,128)(2,1)S(1)}, u32[]{:S(2)}, u32[]{:S(2)}) %collective-permute-start.3) | collective-permute-done | bytes 43040 | tf_op jit(solution)/shard_map/ppermute | solution.py:22
  55.1 0.7 fusion.2
  55.8 0.0 copy-done.1
  55.8 0.0 copy-start.3
  55.8 1.5 fusion.9
  57.3 0.2 pad_bitcast_fusion
  57.6 0.4 copy-done.3
  57.9 29.8 %fusion = f32[1,8,24,5,192]{4,0,3,2,1:T(1,128)S(1)} fusion(bf16[3,3,3,384,192]{3,4,2,1,0:T(8,128)(2,1)S(1)} %copy-done.3, bf16[1,10,26,7,384]{4,2,1,3,0:T(8,128)(2,1)S(1)} %pad_bitcast_fusion), kind=kOutput, calls=%fused_computation.2 | convolution fusion | flops 3822059520 | bytes 6116352 | tf_op jit(solution)/shard_map/conv_general_dilated | solution.py:49
  87.7 0.3 fusion.11
  88.0 2.5 %collective-permute-start.4 = (bf16[8,24,1,192]{3,1,0,2:T(8,128)(2,1)S(1)}, bf16[8,24,1,192]{3,1,0,2:T(8,128)(2,1)S(1)}, u32[]{:S(2)}, u32[]{:S(2)}) collective-permute-start(bf16[8,24,1,192]{3,1,0,2:T(8,128)(2,1)S(1)} %get-tuple-element.11), channel_id=1, source_target_pairs={{0,4},{4,8},{8,12},{1,5},{5,9},{9,13},{2,6},{6,10},{10,14},{3,7},{... | collective-permute-start | bytes 221192 | tf_op jit(solution)/shard_map/ppermute | solution.py:20
  90.5 1.3 collective-permute-start.5
  91.8 0.9 collective-permute-done.4
  92.7 4.3 %collective-permute-done.5 = bf16[8,24,1,192]{3,1,0,2:T(8,128)(2,1)S(1)} collective-permute-done((bf16[8,24,1,192]{3,1,0,2:T(8,128)(2,1)S(1)}, bf16[8,24,1,192]{3,1,0,2:T(8,128)(2,1)S(1)}, u32[]{:S(2)}, u32[]{:S(2)}) %collective-permute-start.5) | collective-permute-done | bytes 73760 | tf_op jit(solution)/shard_map/ppermute | solution.py:22
  97.0 0.1 pad_maximum_fusion.7
  97.1 1.5 %collective-permute-start.6 = (bf16[8,1,7,192]{3,1,0,2:T(2,128)(2,1)S(1)}, bf16[8,1,7,192]{3,1,0,2:T(2,128)(2,1)S(1)}, u32[]{:S(2)}, u32[]{:S(2)}) collective-permute-start(bf16[8,1,7,192]{3,1,0,2:T(2,128)(2,1)S(1)} %get-tuple-element.9), channel_id=1, source_target_pairs={{0,2},{1,3},{4,6},{5,7},{8,10},{9,11},{12,14},{13,15},{16,18},{17,... | collective-permute-start | bytes 64520 | tf_op jit(solution)/shard_map/ppermute | solution.py:20
  98.7 1.3 collective-permute-start.7
  100.0 0.5 collective-permute-done.6
  100.5 4.3 %collective-permute-done.7 = bf16[8,1,7,192]{3,1,0,2:T(2,128)(2,1)S(1)} collective-permute-done((bf16[8,1,7,192]{3,1,0,2:T(2,128)(2,1)S(1)}, bf16[8,1,7,192]{3,1,0,2:T(2,128)(2,1)S(1)}, u32[]{:S(2)}, u32[]{:S(2)}) %collective-permute-start.7) | collective-permute-done | bytes 21536 | tf_op jit(solution)/shard_map/ppermute | solution.py:22
  104.8 0.5 pad_maximum_fusion.1
  105.3 3.5 %copy.33 = bf16[8,26,7,192]{1,0,2,3:T(8,128)(2,1)} copy(bf16[8,26,7,192]{3,1,0,2:T(8,128)(2,1)S(1)} %pad_maximum_fusion.1) | data formatting | bytes 1118208 | tf_op jit(solution)/shard_map/concatenate | solution.py:18
  108.8 0.0 all-gather.3.cloned.1.call-update
  108.8 14.2 %all-gather.3.cloned.1.call-done = bf16[8,26,7,384]{1,0,2,3:T(8,128)(2,1)} async-done(((bf16[8,26,7,192]{1,0,2,3:T(8,128)(2,1)}), bf16[8,26,7,384]{1,0,2,3:T(8,128)(2,1)}) %all-gather.3.cloned.1.call-update) | async-done | bytes 1118224 | tf_op jit(solution)/shard_map/all_gather | solution.py:59
  122.9 9.9 %copy.34 = bf16[8,26,7,384]{3,0,2,1:T(8,128)(2,1)S(1)} copy(bf16[8,26,7,384]{1,0,2,3:T(8,128)(2,1)} %all-gather.3.cloned.1.call-done) | data formatting | bytes 2236416 | tf_op jit(solution)/shard_map/all_gather | solution.py:59
  132.9 0.2 broadcast_in_dim.14
  133.1 0.0 copy-start.4
  133.1 0.4 broadcast_in_dim.15
  133.5 0.0 copy-done
  133.5 0.2 copy-done.4
  133.7 8.0 %add_convert_fusion = bf16[8,48,10,96]{3,0,2,1:T(8,128)(2,1)} fusion(bf16[8,52,14,384]{3,0,2,1:T(8,128)(2,1)S(1)} %bitcast.30, bf16[3,3,384,96]{2,3,1,0:T(8,128)(2,1)S(1)} %copy-done, f32[96]{0:T(128)S(1)} %copy-done.4), kind=kOutput, calls=%fused_computation.12 | convolution fusion | flops 2548776960 | bytes 5874048 | tf_op jit(solution)/shard_map/conv_general_dilated | solution.py:61
  141.7 2.6 %copy.35 = bf16[8,48,5,2,96]{1,0,3,4,2:T(8,128)(2,1)S(1)} copy(bf16[8,48,5,2,96]{4,0,3,2,1:T(8,128)(2,1)} %bitcast.31) | data formatting | bytes 1474560 | tf_op jit(solution)/shard_map/convert_element_type | solution.py:75
  144.4 2.8 %copy.36 = bf16[8,48,5,192]{3,1,2,0:T(8,128)(2,1)} copy(bf16[8,48,5,192]{1,0,3,2:T(8,128)(2,1)S(1)} %bitcast.29) | data formatting | bytes 1474560 | tf_op jit(solution)/shard_map/convert_element_type | solution.py:75
  (5 shorter events, 0.1 us)
Async XLA Ops:
  6.5 126.9 %copy-start = (bf16[3,3,384,96]{2,3,1,0:T(8,128)(2,1)S(1)}, bf16[3,3,384,96]{2,3,1,0:T(8,128)(2,1)}, u32[]{:S(2)}) copy-start(bf16[3,3,384,96]{2,3,1,0:T(8,128)(2,1)} %param.10) | copy-start | bytes 1990660
  6.5 116.4 %all-gather.3.cloned.1.call-start = ((), (), s32[]{:S(2)}) async-start(), calls=%async_computation.1 | async-start | bytes 8257536 | tf_op jit(solution)/shard_map/all_gather | solution.py:59
  10.3 45.5 %copy-start.1 = (f32[384]{0:T(512)S(1)}, f32[384]{0:T(512)}, u32[]{:S(2)}) copy-start(f32[384]{0:T(512)} %param.7) | copy-start | bytes 4612
  35.8 4.9 %collective-permute-start = (bf16[8,24,1,384]{3,1,0,2:T(8,128)(2,1)S(1)}, bf16[8,24,1,384]{3,1,0,2:T(8,128)(2,1)S(1)}, u32[]{:S(2)}, u32[]{:S(2)}) collective-permute-start(bf16[8,24,1,384]{3,1,0,2:T(8,128)(2,1)S(1)} %get-tuple-element.7), channel_id=1, source_target_pairs={{0,4},{4,8},{8,12},{1,5},{5,9},{9,13},{2,6},{6,10},{10,14},{3,7},{... | collective-permute-start | bytes 442376 | tf_op jit(solution)/shard_map/ppermute | solution.py:20
  38.1 7.0 %collective-permute-start.1 = (bf16[8,24,1,384]{3,1,0,2:T(8,128)(2,1)S(1)}, bf16[8,24,1,384]{3,1,0,2:T(8,128)(2,1)S(1)}, u32[]{:S(2)}, u32[]{:S(2)}) collective-permute-start(bf16[8,24,1,384]{3,1,0,2:T(8,128)(2,1)S(1)} %get-tuple-element.8), channel_id=1, source_target_pairs={{4,0},{8,4},{12,8},{5,1},{9,5},{13,9},{6,2},{10,6},{14,10},{7,3},{... | collective-permute-start | bytes 442376 | tf_op jit(solution)/shard_map/ppermute | solution.py:22
  45.3 5.5 %collective-permute-start.2 = (bf16[8,1,7,384]{3,1,0,2:T(2,128)(2,1)S(1)}, bf16[8,1,7,384]{3,1,0,2:T(2,128)(2,1)S(1)}, u32[]{:S(2)}, u32[]{:S(2)}) collective-permute-start(bf16[8,1,7,384]{3,1,0,2:T(2,128)(2,1)S(1)} %get-tuple-element.5), channel_id=1, source_target_pairs={{0,2},{1,3},{4,6},{5,7},{8,10},{9,11},{12,14},{13,15},{16,18},{17,... | collective-permute-start | bytes 129032 | tf_op jit(solution)/shard_map/ppermute | solution.py:20
  48.7 6.4 %collective-permute-start.3 = (bf16[8,1,7,384]{3,1,0,2:T(2,128)(2,1)S(1)}, bf16[8,1,7,384]{3,1,0,2:T(2,128)(2,1)S(1)}, u32[]{:S(2)}, u32[]{:S(2)}) collective-permute-start(bf16[8,1,7,384]{3,1,0,2:T(2,128)(2,1)S(1)} %get-tuple-element.6), channel_id=1, source_target_pairs={{2,0},{3,1},{6,4},{7,5},{10,8},{11,9},{14,12},{15,13},{18,16},{19,... | collective-permute-start | bytes 129032 | tf_op jit(solution)/shard_map/ppermute | solution.py:22
  55.8 2.1 %copy-start.3 = (bf16[3,3,3,384,192]{3,4,2,1,0:T(8,128)(2,1)S(1)}, bf16[3,3,3,384,192]{3,4,2,1,0:T(8,128)(2,1)}, u32[]{:S(2)}) copy-start(bf16[3,3,3,384,192]{3,4,2,1,0:T(8,128)(2,1)} %param.8) | copy-start | bytes 11943940
  57.9 29.8 %copy-start.2 = (f32[192]{0:T(256)S(1)}, f32[192]{0:T(256)}, u32[]{:S(2)}) copy-start(f32[192]{0:T(256)} %param.9) | copy-start | bytes 2308
  88.0 4.7 %collective-permute-start.4 = (bf16[8,24,1,192]{3,1,0,2:T(8,128)(2,1)S(1)}, bf16[8,24,1,192]{3,1,0,2:T(8,128)(2,1)S(1)}, u32[]{:S(2)}, u32[]{:S(2)}) collective-permute-start(bf16[8,24,1,192]{3,1,0,2:T(8,128)(2,1)S(1)} %get-tuple-element.11), channel_id=1, source_target_pairs={{0,4},{4,8},{8,12},{1,5},{5,9},{9,13},{2,6},{6,10},{10,14},{3,7},{... | collective-permute-start | bytes 221192 | tf_op jit(solution)/shard_map/ppermute | solution.py:20
  90.5 6.5 %collective-permute-start.5 = (bf16[8,24,1,192]{3,1,0,2:T(8,128)(2,1)S(1)}, bf16[8,24,1,192]{3,1,0,2:T(8,128)(2,1)S(1)}, u32[]{:S(2)}, u32[]{:S(2)}) collective-permute-start(bf16[8,24,1,192]{3,1,0,2:T(8,128)(2,1)S(1)} %get-tuple-element.12), channel_id=1, source_target_pairs={{4,0},{8,4},{12,8},{5,1},{9,5},{13,9},{6,2},{10,6},{14,10},{7,3},{... | collective-permute-start | bytes 221192 | tf_op jit(solution)/shard_map/ppermute | solution.py:22
  97.1 3.4 %collective-permute-start.6 = (bf16[8,1,7,192]{3,1,0,2:T(2,128)(2,1)S(1)}, bf16[8,1,7,192]{3,1,0,2:T(2,128)(2,1)S(1)}, u32[]{:S(2)}, u32[]{:S(2)}) collective-permute-start(bf16[8,1,7,192]{3,1,0,2:T(2,128)(2,1)S(1)} %get-tuple-element.9), channel_id=1, source_target_pairs={{0,2},{1,3},{4,6},{5,7},{8,10},{9,11},{12,14},{13,15},{16,18},{17,... | collective-permute-start | bytes 64520 | tf_op jit(solution)/shard_map/ppermute | solution.py:20
  98.7 6.1 %collective-permute-start.7 = (bf16[8,1,7,192]{3,1,0,2:T(2,128)(2,1)S(1)}, bf16[8,1,7,192]{3,1,0,2:T(2,128)(2,1)S(1)}, u32[]{:S(2)}, u32[]{:S(2)}) collective-permute-start(bf16[8,1,7,192]{3,1,0,2:T(2,128)(2,1)S(1)} %get-tuple-element.10), channel_id=1, source_target_pairs={{2,0},{3,1},{6,4},{7,5},{10,8},{11,9},{14,12},{15,13},{18,16},{19,... | collective-permute-start | bytes 64520 | tf_op jit(solution)/shard_map/ppermute | solution.py:22
  133.1 0.7 copy-start.4
Sparse Core Ops, SparseCore 0:
  108.9 13.9 all-gather.2
where the time goes:
time: 154 us
  matrix products  37.8 us (25%)
  waiting for transfers between devices  35 us (23%)
  blocking collectives  28.2 us (18%)
  local copies, waits for them, and re-layouts  21.3 us (14%)
  starting transfers between devices  14.8 us (10%)
  between operations  13.6 us (9%)
  other arithmetic  3.28 us (2%)
    conv_general_dilated x1, matrix products, body(): lax.conv_general_dilated(shifted[None], conv_weight, (1, 1, 1), 'VALID',...  29.8 us
    all_to_all x1, blocking collectives, body(): lax.all_to_all(arranged, 'seq', split_axis=1, concat_axis=0, tiled=True)  25.4 us
    ppermute x4, waiting for transfers between devices, extended(): lax.ppermute(head, axis, [((i + 1) % count, i) for i in range(ends)])  17.3 us
    all_gather x1, waiting for transfers between devices, body(): middle_full = lax.all_gather(middle_rim, 'chan', axis=3, tiled=True)  14.2 us
    all_gather x1, local copies, waits for them, and re-layouts, body(): middle_full = lax.all_gather(middle_rim, 'chan', axis=3, tiled=True)  9.9 us
    ppermute x4, starting transfers between devices, extended(): lax.ppermute(tail, axis, [(i, (i + 1) % count) for i in range(ends)])  9.67 us
    conv_general_dilated x1, matrix products, body(): lax.conv_general_dilated(upsampled, upsample_weight, (1, 1), 'VALID', dim...  8.02 us
    convert_element_type x2, local copies, waits for them, and re-layouts, body(): return image.astype(jnp.bfloat16)  5.44 us
  transfers between devices with their start and end apart: 9, of which 9 were waited for; matrix products, arithmetic and copies ran while one was open for 0% of the time, Pallas kernels for 0%

commit v1 on v0

--- a/solution.py
+++ b/solution.py
@@ -38,7 +38,10 @@
     rows_src = FRAMES * ROWS_DEV // seq_count
     whole = lax.all_gather(latents[0], "chan", axis=1, tiled=True)
     arranged = whole.reshape(rows_src, seq_count, COLS_DEV, whole.shape[1])
-    regrouped = lax.all_to_all(arranged, "seq", split_axis=1, concat_axis=0, tiled=True)
+    regrouped = jnp.concatenate(
+        lax.all_to_all(jnp.stack(jnp.split(arranged, lax.axis_size("seq"), axis=1)), "seq", 0, 0),
+        axis=0,
+    )
     full_field = regrouped.reshape(FRAMES, ROWS_DEV, COLS_DEV, whole.shape[1])
     padded = extended(full_field, (("seq", 2), ("tile", 1)), 1)
     field_own = lax.dynamic_slice_in_dim(

time: 154 us -> 157 us (1.019)
  matrix products: 37.8 us -> 35.1 us
  waiting for transfers between devices: 35 us -> 37.5 us
    conv_general_dilated x1, matrix products: 29.8 us -> 27 us  [body(): lax.conv_general_dilated(shifted[None], conv_weight, (1, 1, 1), 'VALID',...]
    ppermute x4, waiting for transfers between devices: 3.52 us -> 6.25 us  [extended(): lax.ppermute(tail, axis, [(i, (i + 1) % count) for i in range(ends)])]
where the time goes in v1:
time: 157 us; the launch traced here: 156 us
  waiting for transfers between devices  37.5 us (24%)
  matrix products  35.1 us (22%)
  blocking collectives  28.2 us (18%)
  local copies, waits for them, and re-layouts  21.4 us (14%)
  starting transfers between devices  15.9 us (10%)
  between operations  13.6 us (9%)
  other arithmetic  4.72 us (3%)
    conv_general_dilated x1, matrix products, body(): lax.conv_general_dilated(shifted[None], conv_weight, (1, 1, 1), 'VALID',...  27 us
    all_to_all x1, blocking collectives, body(): lax.all_to_all(jnp.stack(jnp.split(arranged, lax.axis_size('seq'), axis=1...  25.4 us
    ppermute x4, waiting for transfers between devices, extended(): lax.ppermute(head, axis, [((i + 1) % count, i) for i in range(ends)])  17 us
    all_gather x1, waiting for transfers between devices, body(): middle_full = lax.all_gather(middle_rim, 'chan', axis=3, tiled=True)  14.2 us
    ppermute x4, starting transfers between devices, extended(): lax.ppermute(tail, axis, [(i, (i + 1) % count) for i in range(ends)])  10.7 us
    all_gather x1, local copies, waits for them, and re-layouts, body(): middle_full = lax.all_gather(middle_rim, 'chan', axis=3, tiled=True)  9.9 us
    conv_general_dilated x1, matrix products, body(): lax.conv_general_dilated(upsampled, upsample_weight, (1, 1), 'VALID', dim...  8.02 us
    ppermute x4, waiting for transfers between devices, extended(): lax.ppermute(tail, axis, [(i, (i + 1) % count) for i in range(ends)])  6.25 us
  transfers between devices with their start and end apart: 9, of which 9 were waited for; matrix products, arithmetic and copies ran while one was open for 0% of the time, Pallas kernels for 0%

profile of v1, /device:TPU:0, one launch (start us, length us, event | category | flops | bytes accessed | tf_op | source)
XLA Modules:
  0.0 156.4 jit_solution(91435738804328449)
XLA Ops:
  6.5 2.8 %all-gather = bf16[1,960,384]{1,2,0:T(8,128)(2,1)S(1)} all-gather(bf16[1,960,192]{1,2,0:T(8,128)(2,1)} %param.6), channel_id=2, replica_groups=mesh['groups'=2,'seq'=4,'tile'=2,'chan'=2] {'chan'}, dimensions={2}, use_global_device_ids=true | all-gather | bytes 1105920 | tf_op jit(solution)/shard_map/all_gather | solution.py:39
  9.4 0.4 copy.23
  9.7 0.3 reshape.24
  10.0 0.1 slice_bitcast_fusion.3
  10.2 0.4 pad_maximum_fusion.1
  10.5 0.1 copy.27
  10.6 25.4 %all_to_all.5 = bf16[4,48,1,5,384]{4,1,3,2,0:T(8,128)(2,1)S(1)} all-to-all(bf16[4,48,1,5,384]{4,1,3,2,0:T(8,128)(2,1)S(1)} %copy.27), channel_id=1, replica_groups=mesh['groups'=2,'seq'=4,'tile'=2,'chan'=2] {'seq'}, dimensions={0} | all-to-all | bytes 1474560 | tf_op jit(solution)/shard_map/all_to_all | solution.py:42
  36.0 0.3 copy.28
  36.3 0.4 fusion.12
  36.7 2.3 %collective-permute-start = (bf16[8,24,1,384]{3,2,1,0:T(2,128)(2,1)S(1)}, bf16[8,24,1,384]{3,2,1,0:T(2,128)(2,1)S(1)}, u32[]{:S(2)}, u32[]{:S(2)}) collective-permute-start(bf16[8,24,1,384]{3,2,1,0:T(2,128)(2,1)S(1)} %get-tuple-element.9), channel_id=1, source_target_pairs={{0,4},{4,8},{8,12},{1,5},{5,9},{9,13},{2,6},{6,10},{10,14},{3,7},{... | collective-permute-start | bytes 442376 | tf_op jit(solution)/shard_map/ppermute | solution.py:20
  39.0 0.0 copy-start.1
  39.0 1.3 collective-permute-start.1
  40.3 3.7 %collective-permute-done = bf16[8,24,1,384]{3,2,1,0:T(2,128)(2,1)S(1)} collective-permute-done((bf16[8,24,1,384]{3,2,1,0:T(2,128)(2,1)S(1)}, bf16[8,24,1,384]{3,2,1,0:T(2,128)(2,1)S(1)}, u32[]{:S(2)}, u32[]{:S(2)}) %collective-permute-start) | collective-permute-done | bytes 147488 | tf_op jit(solution)/shard_map/ppermute | solution.py:20
  44.0 4.1 %collective-permute-done.1 = bf16[8,24,1,384]{3,2,1,0:T(2,128)(2,1)S(1)} collective-permute-done((bf16[8,24,1,384]{3,2,1,0:T(2,128)(2,1)S(1)}, bf16[8,24,1,384]{3,2,1,0:T(2,128)(2,1)S(1)}, u32[]{:S(2)}, u32[]{:S(2)}) %collective-permute-start.1) | collective-permute-done | bytes 147488 | tf_op jit(solution)/shard_map/ppermute | solution.py:22
  48.1 0.1 pad_maximum_fusion.5
  48.2 3.4 %collective-permute-start.2 = (bf16[8,1,7,384]{3,2,1,0:T(8,128)(2,1)S(1)}, bf16[8,1,7,384]{3,2,1,0:T(8,128)(2,1)S(1)}, u32[]{:S(2)}, u32[]{:S(2)}) collective-permute-start(bf16[8,1,7,384]{3,2,1,0:T(8,128)(2,1)S(1)} %get-tuple-element.5), channel_id=1, source_target_pairs={{0,2},{1,3},{4,6},{5,7},{8,10},{9,11},{12,14},{13,15},{16,18},{17,... | collective-permute-start | bytes 129032 | tf_op jit(solution)/shard_map/ppermute | solution.py:20
  51.6 1.3 collective-permute-start.3
  52.9 0.4 collective-permute-done.2
  53.3 4.3 %collective-permute-done.3 = bf16[8,1,7,384]{3,2,1,0:T(8,128)(2,1)S(1)} collective-permute-done((bf16[8,1,7,384]{3,2,1,0:T(8,128)(2,1)S(1)}, bf16[8,1,7,384]{3,2,1,0:T(8,128)(2,1)S(1)}, u32[]{:S(2)}, u32[]{:S(2)}) %collective-permute-start.3) | collective-permute-done | bytes 43040 | tf_op jit(solution)/shard_map/ppermute | solution.py:22
  57.6 1.2 fusion.2
  58.9 0.0 copy-start.3
  58.9 1.7 %fusion.9 = bf16[8,26,7,384]{3,2,1,0:T(8,128)(2,1)S(1)} fusion(f32[384]{0:T(512)S(1)} %copy-done.1, f32[8,26,7]{2,1,0:T(8,128)S(1)} %add_rsqrt_fusion, bf16[8,1,7,384]{3,2,1,0:T(8,128)(2,1)S(1)} %collective-permute-done.3, bf16[8,24,1,384]{3,2,1,0:T(2,128)(2,1)S(1)} %collective-permute-done.1, bf16[8,24,5,384]{3,2,1,0:T(8,128)(2,1)S(1)} %bitcast.36, ...), kind=kLoop, calls=%fused_computation.11 | loop fusion | flops 9504768 | bytes 2243776 | tf_op jit(solution)/shard_map/convert_element_type | solution.py:32
  60.6 0.3 pad_bitcast_fusion
  60.8 0.2 copy-done.3
  61.0 27.0 %fusion = f32[1,8,24,5,192]{4,0,3,2,1:T(1,128)S(1)} fusion(bf16[3,3,3,384,192]{3,4,2,1,0:T(8,128)(2,1)S(1)} %copy-done.3, bf16[1,10,26,7,384]{4,3,2,1,0:T(8,128)(2,1)S(1)} %pad_bitcast_fusion), kind=kOutput, calls=%fused_computation.2 | convolution fusion | flops 3822059520 | bytes 6116352 | tf_op jit(solution)/shard_map/conv_general_dilated | solution.py:52
  88.1 0.5 fusion.11
  88.6 0.3 fusion.13
  88.9 3.5 %collective-permute-start.4 = (bf16[8,24,1,192]{3,2,1,0:T(2,128)(2,1)S(1)}, bf16[8,24,1,192]{3,2,1,0:T(2,128)(2,1)S(1)}, u32[]{:S(2)}, u32[]{:S(2)}) collective-permute-start(bf16[8,24,1,192]{3,2,1,0:T(2,128)(2,1)S(1)} %get-tuple-element.15), channel_id=1, source_target_pairs={{0,4},{4,8},{8,12},{1,5},{5,9},{9,13},{2,6},{6,10},{10,14},{3,7},{... | collective-permute-start | bytes 221192 | tf_op jit(solution)/shard_map/ppermute | solution.py:20
  92.3 1.3 collective-permute-start.5
  93.6 1.9 %collective-permute-done.4 = bf16[8,24,1,192]{3,2,1,0:T(2,128)(2,1)S(1)} collective-permute-done((bf16[8,24,1,192]{3,2,1,0:T(2,128)(2,1)S(1)}, bf16[8,24,1,192]{3,2,1,0:T(2,128)(2,1)S(1)}, u32[]{:S(2)}, u32[]{:S(2)}) %collective-permute-start.4) | collective-permute-done | bytes 73760 | tf_op jit(solution)/shard_map/ppermute | solution.py:20
  95.5 4.4 %collective-permute-done.5 = bf16[8,24,1,192]{3,2,1,0:T(2,128)(2,1)S(1)} collective-permute-done((bf16[8,24,1,192]{3,2,1,0:T(2,128)(2,1)S(1)}, bf16[8,24,1,192]{3,2,1,0:T(2,128)(2,1)S(1)}, u32[]{:S(2)}, u32[]{:S(2)}) %collective-permute-start.5) | collective-permute-done | bytes 73760 | tf_op jit(solution)/shard_map/ppermute | solution.py:22
  99.9 0.1 pad_maximum_fusion.8
  100.0 1.6 %collective-permute-start.6 = (bf16[8,1,7,192]{3,2,1,0:T(8,128)(2,1)S(1)}, bf16[8,1,7,192]{3,2,1,0:T(8,128)(2,1)S(1)}, u32[]{:S(2)}, u32[]{:S(2)}) collective-permute-start(bf16[8,1,7,192]{3,2,1,0:T(8,128)(2,1)S(1)} %get-tuple-element.7), channel_id=1, source_target_pairs={{0,2},{1,3},{4,6},{5,7},{8,10},{9,11},{12,14},{13,15},{16,18},{17,... | collective-permute-start | bytes 64520 | tf_op jit(solution)/shard_map/ppermute | solution.py:20
  101.6 1.3 collective-permute-start.7
  102.9 0.3 collective-permute-done.6
  103.1 4.2 %collective-permute-done.7 = bf16[8,1,7,192]{3,2,1,0:T(8,128)(2,1)S(1)} collective-permute-done((bf16[8,1,7,192]{3,2,1,0:T(8,128)(2,1)S(1)}, bf16[8,1,7,192]{3,2,1,0:T(8,128)(2,1)S(1)}, u32[]{:S(2)}, u32[]{:S(2)}) %collective-permute-start.7) | collective-permute-done | bytes 21536 | tf_op jit(solution)/shard_map/ppermute | solution.py:22
  107.4 0.7 pad_maximum_fusion.2
  108.1 3.0 %copy.32 = bf16[8,26,7,192]{1,0,2,3:T(8,128)(2,1)} copy(bf16[8,26,7,192]{3,2,1,0:T(8,128)(2,1)S(1)} %pad_maximum_fusion.2) | data formatting | bytes 1118208 | tf_op jit(solution)/shard_map/concatenate | solution.py:18
  111.1 0.0 all-gather.3.cloned.1.call-update
  111.1 14.2 %all-gather.3.cloned.1.call-done = bf16[8,26,7,384]{1,0,2,3:T(8,128)(2,1)} async-done(((bf16[8,26,7,192]{1,0,2,3:T(8,128)(2,1)}), bf16[8,26,7,384]{1,0,2,3:T(8,128)(2,1)}) %all-gather.3.cloned.1.call-update) | async-done | bytes 1118224 | tf_op jit(solution)/shard_map/all_gather | solution.py:62
  125.3 9.9 %copy.33 = bf16[8,26,7,384]{3,0,2,1:T(8,128)(2,1)S(1)} copy(bf16[8,26,7,384]{1,0,2,3:T(8,128)(2,1)} %all-gather.3.cloned.1.call-done) | data formatting | bytes 2236416 | tf_op jit(solution)/shard_map/all_gather | solution.py:62
  135.2 0.2 broadcast_in_dim.14
  135.4 0.0 copy-start.4
  135.4 0.4 broadcast_in_dim.15
  135.8 0.2 copy-done.4
  136.1 8.0 %add_convert_fusion = bf16[8,48,10,96]{3,0,2,1:T(8,128)(2,1)} fusion(bf16[8,52,14,384]{3,0,2,1:T(8,128)(2,1)S(1)} %bitcast.40, bf16[3,3,384,96]{2,3,1,0:T(8,128)(2,1)S(1)} %copy-done, f32[96]{0:T(128)S(1)} %copy-done.4), kind=kOutput, calls=%fused_computation.12 | convolution fusion | flops 2548776960 | bytes 5874048 | tf_op jit(solution)/shard_map/conv_general_dilated | solution.py:64
  144.1 2.6 %copy.34 = bf16[8,48,5,2,96]{1,0,3,4,2:T(8,128)(2,1)S(1)} copy(bf16[8,48,5,2,96]{4,0,3,2,1:T(8,128)(2,1)} %bitcast.41) | data formatting | bytes 1474560 | tf_op jit(solution)/shard_map/convert_element_type | solution.py:78
  146.7 2.8 %copy.35 = bf16[8,48,5,192]{3,1,2,0:T(8,128)(2,1)} copy(bf16[8,48,5,192]{1,0,3,2:T(8,128)(2,1)S(1)} %bitcast.39) | data formatting | bytes 1474560 | tf_op jit(solution)/shard_map/convert_element_type | solution.py:78
  (7 shorter events, 0.0 us)
Async XLA Ops:
  6.5 129.3 %copy-start = (bf16[3,3,384,96]{2,3,1,0:T(8,128)(2,1)S(1)}, bf16[3,3,384,96]{2,3,1,0:T(8,128)(2,1)}, u32[]{:S(2)}) copy-start(bf16[3,3,384,96]{2,3,1,0:T(8,128)(2,1)} %param.10) | copy-start | bytes 1990660
  6.5 118.8 %all-gather.3.cloned.1.call-start = ((), (), s32[]{:S(2)}) async-start(), calls=%async_computation.1 | async-start | bytes 8257536 | tf_op jit(solution)/shard_map/all_gather | solution.py:62
  36.7 7.3 %collective-permute-start = (bf16[8,24,1,384]{3,2,1,0:T(2,128)(2,1)S(1)}, bf16[8,24,1,384]{3,2,1,0:T(2,128)(2,1)S(1)}, u32[]{:S(2)}, u32[]{:S(2)}) collective-permute-start(bf16[8,24,1,384]{3,2,1,0:T(2,128)(2,1)S(1)} %get-tuple-element.9), channel_id=1, source_target_pairs={{0,4},{4,8},{8,12},{1,5},{5,9},{9,13},{2,6},{6,10},{10,14},{3,7},{... | collective-permute-start | bytes 442376 | tf_op jit(solution)/shard_map/ppermute | solution.py:20
  39.0 19.9 %copy-start.1 = (f32[384]{0:T(512)S(1)}, f32[384]{0:T(512)}, u32[]{:S(2)}) copy-start(f32[384]{0:T(512)} %param.7) | copy-start | bytes 4612
  39.0 9.1 %collective-permute-start.1 = (bf16[8,24,1,384]{3,2,1,0:T(2,128)(2,1)S(1)}, bf16[8,24,1,384]{3,2,1,0:T(2,128)(2,1)S(1)}, u32[]{:S(2)}, u32[]{:S(2)}) collective-permute-start(bf16[8,24,1,384]{3,2,1,0:T(2,128)(2,1)S(1)} %get-tuple-element.10), channel_id=1, source_target_pairs={{4,0},{8,4},{12,8},{5,1},{9,5},{13,9},{6,2},{10,6},{14,10},{7,3},{... | collective-permute-start | bytes 442376 | tf_op jit(solution)/shard_map/ppermute | solution.py:22
  48.2 5.1 %collective-permute-start.2 = (bf16[8,1,7,384]{3,2,1,0:T(8,128)(2,1)S(1)}, bf16[8,1,7,384]{3,2,1,0:T(8,128)(2,1)S(1)}, u32[]{:S(2)}, u32[]{:S(2)}) collective-permute-start(bf16[8,1,7,384]{3,2,1,0:T(8,128)(2,1)S(1)} %get-tuple-element.5), channel_id=1, source_target_pairs={{0,2},{1,3},{4,6},{5,7},{8,10},{9,11},{12,14},{13,15},{16,18},{17,... | collective-permute-start | bytes 129032 | tf_op jit(solution)/shard_map/ppermute | solution.py:20
  51.6 6.0 %collective-permute-start.3 = (bf16[8,1,7,384]{3,2,1,0:T(8,128)(2,1)S(1)}, bf16[8,1,7,384]{3,2,1,0:T(8,128)(2,1)S(1)}, u32[]{:S(2)}, u32[]{:S(2)}) collective-permute-start(bf16[8,1,7,384]{3,2,1,0:T(8,128)(2,1)S(1)} %get-tuple-element.6), channel_id=1, source_target_pairs={{2,0},{3,1},{6,4},{7,5},{10,8},{11,9},{14,12},{15,13},{18,16},{19,... | collective-permute-start | bytes 129032 | tf_op jit(solution)/shard_map/ppermute | solution.py:22
  58.9 2.1 %copy-start.3 = (bf16[3,3,3,384,192]{3,4,2,1,0:T(8,128)(2,1)S(1)}, bf16[3,3,3,384,192]{3,4,2,1,0:T(8,128)(2,1)}, u32[]{:S(2)}) copy-start(bf16[3,3,3,384,192]{3,4,2,1,0:T(8,128)(2,1)} %param.8) | copy-start | bytes 11943940
  61.0 27.0 %copy-start.2 = (f32[192]{0:T(256)S(1)}, f32[192]{0:T(256)}, u32[]{:S(2)}) copy-start(f32[192]{0:T(256)} %param.9) | copy-start | bytes 2308
  88.9 6.6 %collective-permute-start.4 = (bf16[8,24,1,192]{3,2,1,0:T(2,128)(2,1)S(1)}, bf16[8,24,1,192]{3,2,1,0:T(2,128)(2,1)S(1)}, u32[]{:S(2)}, u32[]{:S(2)}) collective-permute-start(bf16[8,24,1,192]{3,2,1,0:T(2,128)(2,1)S(1)} %get-tuple-element.15), channel_id=1, source_target_pairs={{0,4},{4,8},{8,12},{1,5},{5,9},{9,13},{2,6},{6,10},{10,14},{3,7},{... | collective-permute-start | bytes 221192 | tf_op jit(solution)/shard_map/ppermute | solution.py:20
  92.3 7.6 %collective-permute-start.5 = (bf16[8,24,1,192]{3,2,1,0:T(2,128)(2,1)S(1)}, bf16[8,24,1,192]{3,2,1,0:T(2,128)(2,1)S(1)}, u32[]{:S(2)}, u32[]{:S(2)}) collective-permute-start(bf16[8,24,1,192]{3,2,1,0:T(2,128)(2,1)S(1)} %get-tuple-element.16), channel_id=1, source_target_pairs={{4,0},{8,4},{12,8},{5,1},{9,5},{13,9},{6,2},{10,6},{14,10},{7,3},{... | collective-permute-start | bytes 221192 | tf_op jit(solution)/shard_map/ppermute | solution.py:22
  100.0 3.2 %collective-permute-start.6 = (bf16[8,1,7,192]{3,2,1,0:T(8,128)(2,1)S(1)}, bf16[8,1,7,192]{3,2,1,0:T(8,128)(2,1)S(1)}, u32[]{:S(2)}, u32[]{:S(2)}) collective-permute-start(bf16[8,1,7,192]{3,2,1,0:T(8,128)(2,1)S(1)} %get-tuple-element.7), channel_id=1, source_target_pairs={{0,2},{1,3},{4,6},{5,7},{8,10},{9,11},{12,14},{13,15},{16,18},{17,... | collective-permute-start | bytes 64520 | tf_op jit(solution)/shard_map/ppermute | solution.py:20
  101.6 5.8 %collective-permute-start.7 = (bf16[8,1,7,192]{3,2,1,0:T(8,128)(2,1)S(1)}, bf16[8,1,7,192]{3,2,1,0:T(8,128)(2,1)S(1)}, u32[]{:S(2)}, u32[]{:S(2)}) collective-permute-start(bf16[8,1,7,192]{3,2,1,0:T(8,128)(2,1)S(1)} %get-tuple-element.8), channel_id=1, source_target_pairs={{2,0},{3,1},{6,4},{7,5},{10,8},{11,9},{14,12},{15,13},{18,16},{19,... | collective-permute-start | bytes 64520 | tf_op jit(solution)/shard_map/ppermute | solution.py:22
  135.4 0.7 copy-start.4
Sparse Core Ops, SparseCore 0:
  111.2 14.0 all-gather.2
